TPU v7x, 256 devices: a whole 4x4x8 slice. The times are simulated.
256 devices in a mesh: stream: 16 (over y, z_hi, core), span: 16 (over z_lo, x).
Axes of the slice: x: 4, y: 4, z: 8 (z_hi: 2, z_lo: 4; z = z_hi * 4 + z_lo), core: 2. Of those that a mesh axis runs over, the one named last changes fastest.
Arguments:
- velocity_modes: bfloat16 [32, 128, 10, 3, 128], P('stream', 'span'), may hold values from -6 to 6
- cell_weight: float32 [32, 128, 10], P('stream', 'span'), may hold values from 0.001 to 0.01
Outputs:
- convection: float32 [128, 128, 128], replicated
All inputs are finite; a program needn't handle non-finite values.
Results may differ from a plain program's by a relative error of at most 0.0085.
Values may be sent and summed in bfloat16 or wider, within the bound.
A program may use at most 64 MiB of HBM per device.

v0:
```python
import jax
import jax.numpy as jnp
from jax import lax
from jax.sharding import PartitionSpec as P


def with_halo(cells, sides, width):
    for axis, dim in sides:
        count = lax.axis_size(axis)
        ends = count - 1
        head = lax.slice_in_dim(cells, 0, width, axis=dim)
        tail = lax.slice_in_dim(cells, cells.shape[dim] - width, cells.shape[dim], axis=dim)
        cells = jnp.concatenate(
            [
                lax.ppermute(tail, axis, [(i, (i + 1) % count) for i in range(ends)]),
                cells,
                lax.ppermute(head, axis, [((i + 1) % count, i) for i in range(ends)]),
            ],
            axis=dim,
        )
    return cells


def gradient(padded):
    core_x = padded[:, 2:-2]
    deriv_x = (8.0 * (core_x[3:-1] - core_x[1:-3]) - (core_x[4:] - core_x[:-4])) / 12.0
    core_y = padded[2:-2]
    deriv_y = (8.0 * (core_y[:, 3:-1] - core_y[:, 1:-3]) - (core_y[:, 4:] - core_y[:, :-4])) / 12.0
    center = padded[2:-2, 2:-2]
    vertical = jnp.pad(center, ((0, 0), (0, 0), (1, 1), (0, 0), (0, 0)))
    deriv_z = 0.5 * (vertical[:, :, 2:] - vertical[:, :, :-2])
    return jnp.stack([deriv_x, deriv_y, deriv_z])


def shards(velocity_modes, cell_weight):
    padded = with_halo(velocity_modes, (("stream", 0), ("span", 1)), 2)
    grads = gradient(padded.astype(jnp.float32))
    width = velocity_modes.shape[-1]
    cells = velocity_modes.shape[0] * velocity_modes.shape[1] * velocity_modes.shape[2]
    phi_half = velocity_modes.reshape(cells, 3, width)
    grad_cells = grads.reshape(3, cells, 3, width)
    grad_high = grad_cells.astype(jnp.bfloat16)
    grad_low = (grad_cells - grad_high.astype(jnp.float32)).astype(jnp.bfloat16)
    weight_cells = cell_weight.reshape(cells)
    test_count = width * width // width
    block_size = min(8, test_count)
    turns = test_count // block_size

    def one_block(turn_index, result):
        test_start = turn_index * block_size
        phi_test = lax.dynamic_slice_in_dim(phi_half, test_start, block_size, 2)
        quad = jnp.einsum("cbi,acbk->acik", phi_test, grad_high, preferred_element_type=jnp.float32)
        quad = quad + jnp.einsum(
            "cbi,acbk->acik", phi_test, grad_low, preferred_element_type=jnp.float32
        )
        quad = (quad * weight_cells[None, :, None, None]).astype(jnp.bfloat16)
        block_terms = jnp.einsum(
            "caj,acik->ijk", phi_half, quad, preferred_element_type=jnp.float32
        )
        return lax.dynamic_update_slice_in_dim(
            result, block_terms, (turn_index * block_size).astype(jnp.int32), 0
        )

    result = jnp.zeros((test_count, width, width), jnp.float32)
    result = lax.fori_loop(0, turns, one_block, result)
    whole = lax.psum(result.reshape(test_count * width, width), ("stream", "span"))
    return whole.reshape(width, width, width)


def solution(mesh):
    placed = (P("stream", "span", None, None, None), P("stream", "span", None))
    return jax.shard_map(shards, mesh=mesh, in_specs=placed, out_specs=P(), check_vma=False)
```

profile of v0, /device:TPU:97, one launch (start us, length us, event | category | flops | bytes accessed | tf_op | source)
XLA Modules:
  0.0 390.1 jit_solution(13698949483575971565)
XLA Ops:
  6.5 6.7 %collective-permute-start = (bf16[2,8,10,3,128]{4,1,3,2,0:T(8,128)(2,1)}, bf16[2,8,10,3,128]{4,1,3,2,0:T(8,128)(2,1)S(1)}, u32[]{:S(2)}, u32[]{:S(2)}) collective-permute-start(bf16[2,8,10,3,128]{4,1,3,2,0:T(8,128)(2,1)} %param.4), channel_id=1, source_target_pairs={{0,16},{16,32},{32,48},{48,64},{64,80},{80,96},{96,112},{112,128},... | collective-permute-start | bytes 368648 | tf_op jit(solution)/shard_map/ppermute | solution.py:15
  13.2 1.9 collective-permute-start.1
  15.1 0.7 collective-permute-done
  15.9 0.9 constant_dynamic-update-slice_fusion.2
  16.8 6.9 %collective-permute-done.1 = bf16[2,8,10,3,128]{4,1,3,2,0:T(8,128)(2,1)S(1)} collective-permute-done((bf16[2,8,10,3,128]{4,1,3,2,0:T(8,128)(2,1)}, bf16[2,8,10,3,128]{4,1,3,2,0:T(8,128)(2,1)S(1)}, u32[]{:S(2)}, u32[]{:S(2)}) %collective-permute-start.1) | collective-permute-done | bytes 122912 | tf_op jit(solution)/shard_map/ppermute | solution.py:17
  23.8 3.1 collective-permute-start.2
  26.9 4.8 %collective-permute-start.3 = (bf16[6,2,10,3,128]{4,1,3,2,0:T(2,128)(2,1)S(1)}, bf16[6,2,10,3,128]{4,1,3,2,0:T(2,128)(2,1)S(1)}, u32[]{:S(2)}, u32[]{:S(2)}) collective-permute-start(bf16[6,2,10,3,128]{4,1,3,2,0:T(2,128)(2,1)S(1)} %get-tuple-element.131), channel_id=1, source_target_pairs={{1,0},{2,1},{3,2},{4,3},{5,4},{6,5},{7,6},{8,7},{9,8},{10,9},{11,1... | collective-permute-start | bytes 276488 | tf_op jit(solution)/shard_map/ppermute | solution.py:17
  31.8 0.9 copy.8
  32.7 0.8 mul.67
  35.0 4.5 %broadcast_in_dim.3.clone = f32[128,128,128]{2,1,0:T(8,128)} broadcast(f32[]{:T(128)} %constant.37.clone.1), dimensions={} | broadcast | bytes 8388612 | tf_op jit(solution)/shard_map/broadcast_in_dim | solution.py:64
  39.5 55.6 %while.14 = (s32[]{:T(128)}, f32[128,128,128]{2,1,0:T(8,128)}, bf16[160,3,128]{2,0,1:T(8,128)(2,1)S(1)}, bf16[3,160,3,128]{3,2,1,0:T(4,128)(2,1)S(1)}, bf16[3,16...) while((s32[]{:T(128)}, f32[128,128,128]{2,1,0:T(8,128)}, ...), condition=%wide.wide.region_1.2_spmd, body=%wide.wide.region_0.1_spmd.sunk | while | flops 133201928 | bytes 11377443 | solution.py:65
  40.2 0.6 fusion.44
  40.7 1.2 convolution_bitcast_fusion.3
  42.1 0.8 constant_dynamic-update-slice_fusion.6
  44.2 1.2 convolution_bitcast_fusion.3
  45.6 0.8 constant_dynamic-update-slice_fusion.6
  47.7 1.2 convolution_bitcast_fusion.3
  49.1 0.8 constant_dynamic-update-slice_fusion.6
  50.0 0.6 fusion.45
  51.2 1.2 convolution_bitcast_fusion.3
  52.5 0.8 constant_dynamic-update-slice_fusion.6
  54.6 1.2 convolution_bitcast_fusion.3
  56.0 0.8 constant_dynamic-update-slice_fusion.6
  58.1 1.2 convolution_bitcast_fusion.3
  59.5 0.8 constant_dynamic-update-slice_fusion.6
  61.6 1.2 convolution_bitcast_fusion.3
  62.9 0.8 constant_dynamic-update-slice_fusion.6
  65.1 1.2 convolution_bitcast_fusion.3
  66.4 0.8 constant_dynamic-update-slice_fusion.6
  68.5 1.2 convolution_bitcast_fusion.3
  69.9 0.8 constant_dynamic-update-slice_fusion.6
  72.0 1.2 convolution_bitcast_fusion.3
  73.4 0.8 constant_dynamic-update-slice_fusion.6
  75.5 1.2 convolution_bitcast_fusion.3
  76.8 0.8 constant_dynamic-update-slice_fusion.6
  78.9 1.2 convolution_bitcast_fusion.3
  80.3 0.8 constant_dynamic-update-slice_fusion.6
  82.4 1.2 convolution_bitcast_fusion.3
  83.8 0.8 constant_dynamic-update-slice_fusion.6
  85.9 1.2 convolution_bitcast_fusion.3
  87.2 0.8 constant_dynamic-update-slice_fusion.6
  89.4 1.2 convolution_bitcast_fusion.3
  90.7 0.8 constant_dynamic-update-slice_fusion.6
  91.7 0.6 fusion.45
  92.8 1.2 convolution_bitcast_fusion.3
  94.2 0.8 constant_dynamic-update-slice_fusion.6
  95.1 280.3 %all-reduce.3.cloned.1.call-done = f32[128,128,128]{2,1,0:T(8,128)} async-done(((f32[128,128,128]{2,1,0:T(8,128)}), f32[128,128,128]{2,1,0:T(8,128)}) %all-reduce.3.cloned.1.call-update) | async-done | bytes 8388624 | tf_op jit(solution)/shard_map/psum | solution.py:66
  375.4 7.9 %copy.73 = f32[128,128,128]{2,1,0:T(8,128)} copy(f32[128,128,128]{2,1,0:T(8,128)} %all-reduce.3.cloned.1.call-done) | data formatting | bytes 16777216
  (77 shorter events, 23.1 us)
Async XLA Ops:
  6.5 368.8 %all-reduce.3.cloned.1.call-start = ((), (), s32[]{:S(2)}) async-start(), calls=%async_computation | async-start | bytes 16777216 | tf_op jit(solution)/shard_map/psum | solution.py:66
  6.5 9.3 %collective-permute-start = (bf16[2,8,10,3,128]{4,1,3,2,0:T(8,128)(2,1)}, bf16[2,8,10,3,128]{4,1,3,2,0:T(8,128)(2,1)S(1)}, u32[]{:S(2)}, u32[]{:S(2)}) collective-permute-start(bf16[2,8,10,3,128]{4,1,3,2,0:T(8,128)(2,1)} %param.4), channel_id=1, source_target_pairs={{0,16},{16,32},{32,48},{48,64},{64,80},{80,96},{96,112},{112,128},... | collective-permute-start | bytes 368648 | tf_op jit(solution)/shard_map/ppermute | solution.py:15
  13.2 10.4 %collective-permute-start.1 = (bf16[2,8,10,3,128]{4,1,3,2,0:T(8,128)(2,1)}, bf16[2,8,10,3,128]{4,1,3,2,0:T(8,128)(2,1)S(1)}, u32[]{:S(2)}, u32[]{:S(2)}) collective-permute-start(bf16[2,8,10,3,128]{4,1,3,2,0:T(8,128)(2,1)} %param.4), channel_id=1, source_target_pairs={{16,0},{32,16},{48,32},{64,48},{80,64},{96,80},{112,96},{128,112},... | collective-permute-start | bytes 368648 | tf_op jit(solution)/shard_map/ppermute | solution.py:17
  23.8 9.8 %collective-permute-start.2 = (bf16[6,2,10,3,128]{4,1,3,2,0:T(2,128)(2,1)S(1)}, bf16[6,2,10,3,128]{4,1,3,2,0:T(2,128)(2,1)S(1)}, u32[]{:S(2)}, u32[]{:S(2)}) collective-permute-start(bf16[6,2,10,3,128]{4,1,3,2,0:T(2,128)(2,1)S(1)} %get-tuple-element.130), channel_id=1, source_target_pairs={{0,1},{1,2},{2,3},{3,4},{4,5},{5,6},{6,7},{7,8},{8,9},{9,10},{10,1... | collective-permute-start | bytes 276488 | tf_op jit(solution)/shard_map/ppermute | solution.py:15
  26.9 6.7 %collective-permute-start.3 = (bf16[6,2,10,3,128]{4,1,3,2,0:T(2,128)(2,1)S(1)}, bf16[6,2,10,3,128]{4,1,3,2,0:T(2,128)(2,1)S(1)}, u32[]{:S(2)}, u32[]{:S(2)}) collective-permute-start(bf16[6,2,10,3,128]{4,1,3,2,0:T(2,128)(2,1)S(1)} %get-tuple-element.131), channel_id=1, source_target_pairs={{1,0},{2,1},{3,2},{4,3},{5,4},{6,5},{7,6},{8,7},{9,8},{10,9},{11,1... | collective-permute-start | bytes 276488 | tf_op jit(solution)/shard_map/ppermute | solution.py:17
Sparse Core Ops, SparseCore 0:
  95.2 280.1 all-reduce.2
where the time goes:
time: 390 us
  waiting for transfers between devices  288 us (74%)
  matrix products  36.9 us (9%)
  local copies, waits for them, and re-layouts  33.7 us (9%)
  starting transfers between devices  16.6 us (4%)
  between operations  13.5 us (3%)
    psum x1, waiting for transfers between devices, shards(): lax.psum(result.reshape(test_count * width, width), ('stream', 'span'))  280 us
    dot_general x16, matrix products, one_block(): jnp.einsum('caj,acik->ijk', phi_half, quad, preferred_element_type=jnp.fl...  18.4 us
    dynamic_update_slice x32, local copies, waits for them, and re-layouts, one_block(): lax.dynamic_update_slice_in_dim(result, block_terms, (turn_index * block_...  16.6 us
    ppermute x2, starting transfers between devices, with_halo(): lax.ppermute(tail, axis, [(i, (i + 1) % count) for i in range(ends)])  9.79 us
    unnamed x4, local copies, waits for them, and re-layouts  9.77 us
    dot_general x16, matrix products, one_block(): jnp.einsum('cbi,acbk->acik', phi_test, grad_high, preferred_element_type=...  9.23 us
    dot_general x16, matrix products, one_block(): jnp.einsum('cbi,acbk->acik', phi_test, grad_low, preferred_element_type=j...  9.22 us
  transfers between devices with their start and end apart: 5, of which 3 were waited for; matrix products, arithmetic and copies ran while one was open for 1% of the time, Pallas kernels for 0%

commit v1 on v0

--- a/solution.py
+++ b/solution.py
@@ -63,7 +63,8 @@
 
     result = jnp.zeros((test_count, width, width), jnp.float32)
     result = lax.fori_loop(0, turns, one_block, result)
-    whole = lax.psum(result.reshape(test_count * width, width), ("stream", "span"))
+    one_axis = lax.psum(result.reshape(test_count * width, width), "span")
+    whole = lax.psum(one_axis, "stream")
     return whole.reshape(width, width, width)
 
 

time: 390 us -> 699 us (1.79)
  the two profiles are of different devices: /device:TPU:97 before, /device:TPU:2 now
where the time goes in v1:
time: 699 us
  waiting for transfers between devices  604 us (86%)
  matrix products  36.9 us (5%)
  local copies, waits for them, and re-layouts  33.7 us (5%)
  between operations  13.5 us (2%)
  starting transfers between devices  8.92 us (1%)
    psum x1, waiting for transfers between devices, shards(): whole = lax.psum(one_axis, 'stream')  383 us
    psum x1, waiting for transfers between devices, shards(): one_axis = lax.psum(result.reshape(test_count * width, width), 'span')  211 us
    dot_general x16, matrix products, one_block(): jnp.einsum('caj,acik->ijk', phi_half, quad, preferred_element_type=jnp.fl...  18.4 us
    dynamic_update_slice x32, local copies, waits for them, and re-layouts, one_block(): lax.dynamic_update_slice_in_dim(result, block_terms, (turn_index * block_...  16.6 us
  transfers between devices with their start and end apart: 6, of which 4 were waited for; matrix products, arithmetic and copies ran while one was open for 0% of the time, Pallas kernels for 0%

profile of v1, /device:TPU:2, one launch (start us, length us, event | category | flops | bytes accessed | tf_op | source)
XLA Modules:
  0.0 699.0 jit_solution(6642513552538497321)
XLA Ops:
  6.5 1.7 collective-permute-start
  8.3 1.3 collective-permute-start.1
  9.6 0.9 constant_dynamic-update-slice_fusion.2
  10.5 8.2 %collective-permute-done.1 = bf16[2,8,10,3,128]{4,1,3,2,0:T(8,128)(2,1)S(1)} collective-permute-done((bf16[2,8,10,3,128]{4,1,3,2,0:T(8,128)(2,1)}, bf16[2,8,10,3,128]{4,1,3,2,0:T(8,128)(2,1)S(1)}, u32[]{:S(2)}, u32[]{:S(2)}) %collective-permute-start.1) | collective-permute-done | bytes 122912 | tf_op jit(solution)/shard_map/ppermute | solution.py:17
  18.8 3.4 collective-permute-start.2
  22.3 2.4 collective-permute-start.3
  24.7 0.9 copy.7
  25.7 0.8 mul.67
  26.5 2.2 collective-permute-done.3
  30.1 4.5 broadcast_in_dim.3.clone
  34.6 55.6 %while.14 = (s32[]{:T(128)}, f32[128,128,128]{2,1,0:T(8,128)}, bf16[160,3,128]{2,0,1:T(8,128)(2,1)S(1)}, bf16[3,160,3,128]{3,2,1,0:T(4,128)(2,1)S(1)}, bf16[3,16...) while((s32[]{:T(128)}, f32[128,128,128]{2,1,0:T(8,128)}, ...), condition=%wide.wide.region_1.2_spmd, body=%wide.wide.region_0.1_spmd.sunk | while | flops 133201928 | bytes 11377443 | solution.py:65
  35.9 1.2 convolution_bitcast_fusion.3
  37.2 0.8 constant_dynamic-update-slice_fusion.6
  39.3 1.2 convolution_bitcast_fusion.3
  40.7 0.8 constant_dynamic-update-slice_fusion.6
  42.8 1.2 convolution_bitcast_fusion.3
  44.2 0.8 constant_dynamic-update-slice_fusion.6
  45.1 0.6 fusion.45
  46.3 1.2 convolution_bitcast_fusion.3
  47.6 0.8 constant_dynamic-update-slice_fusion.6
  49.7 1.2 convolution_bitcast_fusion.3
  51.1 0.8 constant_dynamic-update-slice_fusion.6
  53.2 1.2 convolution_bitcast_fusion.3
  54.6 0.8 constant_dynamic-update-slice_fusion.6
  55.5 0.6 fusion.45
  56.7 1.2 convolution_bitcast_fusion.3
  58.1 0.8 constant_dynamic-update-slice_fusion.6
  60.2 1.2 convolution_bitcast_fusion.3
  61.5 0.8 constant_dynamic-update-slice_fusion.6
  63.6 1.2 convolution_bitcast_fusion.3
  65.0 0.8 constant_dynamic-update-slice_fusion.6
  67.1 1.2 convolution_bitcast_fusion.3
  68.5 0.8 constant_dynamic-update-slice_fusion.6
  70.6 1.2 convolution_bitcast_fusion.3
  71.9 0.8 constant_dynamic-update-slice_fusion.6
  74.1 1.2 convolution_bitcast_fusion.3
  75.4 0.8 constant_dynamic-update-slice_fusion.6
  77.5 1.2 convolution_bitcast_fusion.3
  78.9 0.8 constant_dynamic-update-slice_fusion.6
  81.0 1.2 convolution_bitcast_fusion.3
  82.4 0.8 constant_dynamic-update-slice_fusion.6
  84.5 1.2 convolution_bitcast_fusion.3
  85.8 0.8 constant_dynamic-update-slice_fusion.6
  87.9 1.2 convolution_bitcast_fusion.3
  89.3 0.8 constant_dynamic-update-slice_fusion.6
  90.2 210.8 %all-reduce.4.cloned.1.call-done = f32[16384,128]{1,0:T(8,128)} async-done(((f32[16384,128]{1,0:T(8,128)}), f32[16384,128]{1,0:T(8,128)}) %all-reduce.4.cloned.1.call-update) | async-done | bytes 8388624 | tf_op jit(solution)/shard_map/psum | solution.py:66
  301.0 383.2 %all-reduce.6.cloned.1.call-done = f32[128,128,128]{2,1,0:T(8,128)} async-done(((f32[128,128,128]{2,1,0:T(8,128)}), f32[128,128,128]{2,1,0:T(8,128)}) %all-reduce.6.cloned.1.call-update) | async-done | bytes 8388624 | tf_op jit(solution)/shard_map/psum | solution.py:67
  684.3 7.9 %copy.73 = f32[128,128,128]{2,1,0:T(8,128)} copy(f32[128,128,128]{2,1,0:T(8,128)} %all-reduce.6.cloned.1.call-done) | data formatting | bytes 16777216
  (80 shorter events, 23.8 us)
Async XLA Ops:
  6.5 294.5 %all-reduce.4.cloned.1.call-start = ((), (), s32[]{:S(2)}) async-start(), calls=%async_computation | async-start | bytes 16777216 | tf_op jit(solution)/shard_map/psum | solution.py:66
  6.5 3.0 collective-permute-start
  8.3 10.4 %collective-permute-start.1 = (bf16[2,8,10,3,128]{4,1,3,2,0:T(8,128)(2,1)}, bf16[2,8,10,3,128]{4,1,3,2,0:T(8,128)(2,1)S(1)}, u32[]{:S(2)}, u32[]{:S(2)}) collective-permute-start(bf16[2,8,10,3,128]{4,1,3,2,0:T(8,128)(2,1)} %param.4), channel_id=1, source_target_pairs={{16,0},{32,16},{48,32},{64,48},{80,64},{96,80},{112,96},{128,112},... | collective-permute-start | bytes 368648 | tf_op jit(solution)/shard_map/ppermute | solution.py:17
  18.8 7.6 %collective-permute-start.2 = (bf16[6,2,10,3,128]{4,1,3,2,0:T(2,128)(2,1)S(1)}, bf16[6,2,10,3,128]{4,1,3,2,0:T(2,128)(2,1)S(1)}, u32[]{:S(2)}, u32[]{:S(2)}) collective-permute-start(bf16[6,2,10,3,128]{4,1,3,2,0:T(2,128)(2,1)S(1)} %get-tuple-element.130), channel_id=1, source_target_pairs={{0,1},{1,2},{2,3},{3,4},{4,5},{5,6},{6,7},{7,8},{8,9},{9,10},{10,1... | collective-permute-start | bytes 276488 | tf_op jit(solution)/shard_map/ppermute | solution.py:15
  22.3 6.4 collective-permute-start.3
  90.2 594.1 %all-reduce.6.cloned.1.call-start = ((), (), s32[]{:S(2)}) async-start(), calls=%async_computation.1 | async-start | bytes 16777216 | tf_op jit(solution)/shard_map/psum | solution.py:67
Sparse Core Ops, SparseCore 0:
  90.3 210.6 all-reduce.3
  303.7 380.5 all-reduce.5
